TPU v7x, 512 devices: a whole 4x8x8 slice. The times are simulated.
512 devices in a mesh: mem: 16 (over z, core), head: 8 (over y), span: 4 (over x).
Axes of the slice: x: 4, y: 8, z: 8, core: 2. Of those that a mesh axis runs over, the one named last changes fastest.
Arguments:
- query: bfloat16 [4, 2048, 8, 8, 128], P('span', 'mem', 'head'), may hold values from -6 to 6
- new_keys: bfloat16 [4, 2048, 8, 128], P('span', 'mem', 'head'), may hold values from -6 to 6
- new_values: bfloat16 [4, 2048, 8, 128], P('span', 'mem', 'head'), may hold values from -5 to 5
- memory_keys: bfloat16 [512, 128, 8, 128], P('mem', None, 'head'), may hold values from -5 to 5
- memory_values: bfloat16 [512, 128, 8, 128], P('mem', None, 'head'), may hold values from -5 to 5
- retrieved: int32 [4, 8, 16], P('span', 'head'), may hold values from 0 to 511, as said below
Outputs:
- attended: bfloat16 [4, 2048, 8192], P('span', ('mem', 'head'))
Inputs may be any that keep to these rules, and one draw needn't show every extreme that they name: Each list retrieved[b, h, :] names 16 different units. The units o * 32 to (o + 1) * 32 - 1 appear at most 3 times in one list, and in every list some o has exactly 3.
All inputs are finite; a program needn't handle non-finite values.
Results may differ from a plain program's by a relative error of at most 0.005.
Values may be sent and summed in bfloat16 or wider, within the bound.
A program may use at most 64 MiB of HBM per device.

v0:
```python
import math
import jax
import jax.numpy as jnp
from jax import lax
from jax.sharding import PartitionSpec as P

NEG = -1e30


def shifted(value, axis, steps):
    count = lax.axis_size(axis)
    first, last = (max(0, -steps), min(count, count - steps))
    return lax.ppermute(value, axis, [(source, source + steps) for source in range(first, last)])


def local(query, new_keys, new_values, memory_keys, memory_values, retrieved):
    queries = query[0]
    row_count, head_count, group_size, head_width = queries.shape
    score_scale = 1.0 / math.sqrt(head_width)
    mem_count = lax.axis_size("mem")
    mem_index = lax.axis_index("mem")
    block_index = lax.axis_index("span")
    row_position = mem_index * row_count + jnp.arange(row_count, dtype=jnp.int32)

    def update(carry_state, key_pair, key_mask):
        old_peak, old_total, old_accum = carry_state
        scores = (
            jnp.einsum("rhgd,khd->rhgk", queries, key_pair[0], preferred_element_type=jnp.float32)
            * score_scale
        )
        scores = jnp.where(key_mask, scores, NEG)
        new_peak = jnp.maximum(old_peak, jnp.max(scores, axis=-1))
        weights = jnp.where(key_mask, jnp.exp(scores - new_peak[..., None]), 0.0)
        factor = jnp.exp(old_peak - new_peak)
        new_total = old_total * factor + jnp.sum(weights, axis=-1)
        new_accum = old_accum * factor[..., None] + jnp.einsum(
            "rhgk,khd->rhgd",
            weights.astype(jnp.bfloat16),
            key_pair[1],
            preferred_element_type=jnp.float32,
        )
        return (new_peak, new_total, new_accum)

    def sweep(carry_state, key_pair, first_key, mask_maker):
        key_count = key_pair.shape[1]
        step_size = math.gcd(key_count, 512)

        def advance(step_index, loop_state):
            sub_pair = lax.dynamic_slice_in_dim(key_pair, step_index * step_size, step_size, 1)
            key_position = (
                first_key + step_index * step_size + jnp.arange(step_size, dtype=jnp.int32)
            )
            return update(loop_state, sub_pair, mask_maker(key_position))

        return lax.fori_loop(0, key_count // step_size, advance, carry_state)

    def current_mask(key_position):
        return (key_position[None, :] <= row_position[:, None])[:, None, None, :]

    def prior_mask(key_position):
        return ((key_position[None, :] > row_position[:, None]) & (block_index > 0))[
            :, None, None, :
        ]

    def full_mask(key_position):
        return jnp.ones((1, 1, 1, key_position.shape[0]), bool)

    carry_state = (
        jnp.full((row_count, head_count, group_size), NEG, jnp.float32),
        jnp.zeros((row_count, head_count, group_size), jnp.float32),
        jnp.zeros((row_count, head_count, group_size, head_width), jnp.float32),
    )
    own_pair = jnp.stack([new_keys[0], new_values[0]])
    prior_pair = shifted(own_pair, "span", 1)
    loop_state = carry_state
    first_key = jnp.int32(0)
    loop_state = sweep(
        loop_state, lax.all_gather(own_pair, "mem", axis=1, tiled=True), first_key, current_mask
    )
    carry_state = sweep(
        loop_state, lax.all_gather(prior_pair, "mem", axis=1, tiled=True), first_key, prior_mask
    )
    unit_lists = retrieved[0]
    list_length = unit_lists.shape[1]
    units_dev = memory_keys.shape[0]
    unit_length = memory_keys.shape[1]
    owners = unit_lists // units_dev
    local_units = unit_lists % units_dev
    owned_here = owners == mem_index
    capacity = max(3, 2 * list_length // mem_count)
    ranking = jnp.cumsum(owned_here.astype(jnp.int32), axis=1) - 1
    slot_range = jnp.arange(capacity, dtype=jnp.int32)
    matches = owned_here[:, :, None] & (ranking[:, :, None] == slot_range[None, None, :])
    picked_units = jnp.sum(jnp.where(matches, local_units[:, :, None], 0), axis=1)
    gathered_pair = []
    for source_array in (memory_keys, memory_values):
        per_head = [source_array[picked_units[0], :, 0, :]]
        gathered_pair.append(jnp.stack(per_head, axis=2))
    block_pair = jnp.stack(gathered_pair).reshape(2, capacity * unit_length, head_count, head_width)
    gathered = lax.all_gather(block_pair, "mem", axis=1, tiled=True)
    gathered = gathered.reshape(2, mem_count * capacity, unit_length, head_count, head_width)
    entry_range = jnp.arange(list_length, dtype=jnp.int32)
    earlier = entry_range[None, :] < entry_range[:, None]
    same_owner = owners[:, :, None] == owners[:, None, :]
    owner_rank = jnp.sum((same_owner & earlier[None, :, :]).astype(jnp.int32), axis=2)
    slot_index = owners * capacity + owner_rank
    live_heads = [gathered[:, :, :, 0, :][:, slot_index[0]]]
    live_pair = jnp.stack(live_heads, axis=3).reshape(
        2, list_length * unit_length, head_count, head_width
    )
    carry_state = sweep(carry_state, live_pair, 0, full_mask)
    final_peak, final_total, final_accum = carry_state
    attended = (final_accum / final_total[..., None]).astype(jnp.bfloat16)
    attended = attended.reshape(row_count, head_count * group_size * head_width)
    moved = lax.all_to_all(attended, "head", split_axis=0, concat_axis=1, tiled=True)
    return moved[None]


def solution(mesh):
    return jax.shard_map(
        local,
        mesh=mesh,
        in_specs=(
            P("span", "mem", "head", None, None),
            P("span", "mem", "head", None),
            P("span", "mem", "head", None),
            P("mem", None, "head", None),
            P("mem", None, "head", None),
            P("span", "head", None),
        ),
        out_specs=P("span", ("mem", "head"), None),
        check_vma=False,
    )
```

profile of v0, /device:TPU:1, one launch (start us, length us, event | category | flops | bytes accessed | tf_op | source)
XLA Modules:
  0.0 191.3 jit_solution(4977924991710813457)
XLA Ops:
  6.5 0.8 constant_dynamic-update-slice_fusion.1
  7.4 0.8 constant_dynamic-update-slice_fusion
  8.2 0.6 copy-done.1
  8.8 3.9 %collective-permute-start = (bf16[2,128,1,128]{3,1,2,0:T(8,128)(2,1)}, bf16[2,128,1,128]{3,1,2,0:T(8,128)(2,1)S(1)}, u32[]{:S(2)}, u32[]{:S(2)}) collective-permute-start(bf16[2,128,1,128]{3,1,2,0:T(8,128)(2,1)} %copy-done.1), channel_id=1, source_target_pairs={{0,1},{1,2},{2,3},{4,5},{5,6},{6,7},{8,9},{9,10},{10,11},{12,13},{... | collective-permute-start | bytes 196616 | tf_op jit(solution)/shard_map/ppermute | solution.py:13
  12.8 1.6 collective-permute-done
  14.4 0.6 copy-done.2
  15.1 0.7 copy.60
  16.0 0.7 and_select_fusion.2
  16.7 0.7 broadcast_compare_fusion.1
  18.1 1.8 gather_fusion.1
  19.9 0.7 pad_maximum_fusion
  20.7 0.7 fusion.64
  21.3 1.0 copy.81
  22.7 34.6 %all-gather.4.cloned.1.call-done = bf16[2,2048,1,128]{3,1,2,0:T(8,128)(2,1)} async-done(((bf16[2,128,1,128]{3,1,2,0:T(8,128)(2,1)}), bf16[2,2048,1,128]{3,1,2,0:T(8,128)(2,1)}) %all-gather.4.cloned.1.call-update) | async-done | bytes 1048592 | tf_op jit(solution)/shard_map/all_gather | solution.py:78
  57.3 18.6 %while.57 = (s32[]{:T(128)}, f32[128,1,8]{0,2,1:T(8,128)S(1)}, f32[128,1,8]{0,2,1:T(8,128)S(1)}, f32[128,1,8,128]{0,3,2,1:T(8,128)}, bf16[2,2048,1,128]{3,1,2,0:...) while((s32[]{:T(128)}, f32[128,1,8]{0,2,1:T(8,128)S(1)}, ...), condition=%wide.region_3.4_spmd.clone, body=%wide.region_0.3_spmd.clone.sunk | while | flops 275716736 | bytes 8197327 | solution.py:55
  57.5 1.4 fusion.89
  58.8 2.4 %fusion.92 = f32[128,1,8,128]{0,3,2,1:T(8,128)} fusion(f32[512,128,8]{1,0,2:T(8,128)S(1)} %get-tuple-element.707, f32[128,8]{0,1:T(8,128)S(1)} %bitcast.263, pred[128,512]{0,1:T(8,128)(4,1)S(1)} %broadcast_compare_fusion.3, f32[128,1,8,128]{0,3,2,1:T(8,128)} %get-tuple-element.724, f32[128,8]{0,1:T(8,128)S(1)} %get-tuple-element.708, ...), kind=kOutput, calls=%fused_computation.61.clone.1 | convolution fusion | flops 137232384 | bytes 3350537 | tf_op jit(solution)/shard_map/while/body/eval_jaxpr/rhgk,khd->rhgd/dot_general | solution.py:36
  61.9 1.4 fusion.89
  63.3 2.6 %fusion.92 = f32[128,1,8,128]{0,3,2,1:T(8,128)} fusion(f32[512,128,8]{1,0,2:T(8,128)S(1)} %get-tuple-element.707, f32[128,8]{0,1:T(8,128)S(1)} %bitcast.263, pred[128,512]{0,1:T(8,128)(4,1)S(1)} %broadcast_compare_fusion.3, f32[128,1,8,128]{0,3,2,1:T(8,128)} %get-tuple-element.724, f32[128,8]{0,1:T(8,128)S(1)} %get-tuple-element.708, ...), kind=kOutput, calls=%fused_computation.61.clone.1 | convolution fusion | flops 137232384 | bytes 3350537 | tf_op jit(solution)/shard_map/while/body/eval_jaxpr/rhgk,khd->rhgd/dot_general | solution.py:36
  66.7 1.4 fusion.89
  68.0 2.6 %fusion.92 = f32[128,1,8,128]{0,3,2,1:T(8,128)} fusion(f32[512,128,8]{1,0,2:T(8,128)S(1)} %get-tuple-element.707, f32[128,8]{0,1:T(8,128)S(1)} %bitcast.263, pred[128,512]{0,1:T(8,128)(4,1)S(1)} %broadcast_compare_fusion.3, f32[128,1,8,128]{0,3,2,1:T(8,128)} %get-tuple-element.724, f32[128,8]{0,1:T(8,128)S(1)} %get-tuple-element.708, ...), kind=kOutput, calls=%fused_computation.61.clone.1 | convolution fusion | flops 137232384 | bytes 3350537 | tf_op jit(solution)/shard_map/while/body/eval_jaxpr/rhgk,khd->rhgd/dot_general | solution.py:36
  71.4 1.4 fusion.89
  72.7 2.6 %fusion.92 = f32[128,1,8,128]{0,3,2,1:T(8,128)} fusion(f32[512,128,8]{1,0,2:T(8,128)S(1)} %get-tuple-element.707, f32[128,8]{0,1:T(8,128)S(1)} %bitcast.263, pred[128,512]{0,1:T(8,128)(4,1)S(1)} %broadcast_compare_fusion.3, f32[128,1,8,128]{0,3,2,1:T(8,128)} %get-tuple-element.724, f32[128,8]{0,1:T(8,128)S(1)} %get-tuple-element.708, ...), kind=kOutput, calls=%fused_computation.61.clone.1 | convolution fusion | flops 137232384 | bytes 3350537 | tf_op jit(solution)/shard_map/while/body/eval_jaxpr/rhgk,khd->rhgd/dot_general | solution.py:36
  75.9 23.7 %all-gather.6.cloned.1.call-done = bf16[2,2048,1,128]{3,1,2,0:T(8,128)(2,1)} async-done(((bf16[2,128,1,128]{3,1,2,0:T(8,128)(2,1)}), bf16[2,2048,1,128]{3,1,2,0:T(8,128)(2,1)}) %all-gather.6.cloned.1.call-update) | async-done | bytes 1048592 | tf_op jit(solution)/shard_map/all_gather | solution.py:81
  99.6 18.8 %while.56 = (s32[]{:T(128)}, f32[128,1,8]{0,2,1:T(8,128)S(1)}, f32[128,1,8]{0,2,1:T(8,128)S(1)}, f32[128,1,8,128]{0,3,2,1:T(8,128)}, pred[]{:T(512)}, /*index=5*...) while((s32[]{:T(128)}, f32[128,1,8]{0,2,1:T(8,128)S(1)}, ...), condition=%wide.region_7.8_spmd.clone, body=%wide.region_4.7_spmd.clone.sunk | while | flops 275648128 | bytes 8197324 | solution.py:55
  99.7 1.4 fusion.84
  101.1 2.6 %fusion.87 = f32[128,1,8,128]{0,3,2,1:T(8,128)} fusion(f32[512,128,8]{1,0,2:T(8,128)S(1)} %get-tuple-element.696, f32[128,8]{0,1:T(8,128)S(1)} %bitcast.261, pred[128,512]{0,1:T(8,128)(4,1)S(1)} %compare_and_fusion.2, f32[128,1,8,128]{0,3,2,1:T(8,128)} %get-tuple-element.761, f32[128,8]{0,1:T(8,128)S(1)} %get-tuple-element.697, ...), kind=kOutput, calls=%fused_computation.32.clone.1 | convolution fusion | flops 137101312 | bytes 3350536 | tf_op jit(solution)/shard_map/while/body/eval_jaxpr/rhgk,khd->rhgd/dot_general | solution.py:36
  104.4 1.4 fusion.84
  105.8 2.6 %fusion.87 = f32[128,1,8,128]{0,3,2,1:T(8,128)} fusion(f32[512,128,8]{1,0,2:T(8,128)S(1)} %get-tuple-element.696, f32[128,8]{0,1:T(8,128)S(1)} %bitcast.261, pred[128,512]{0,1:T(8,128)(4,1)S(1)} %compare_and_fusion.2, f32[128,1,8,128]{0,3,2,1:T(8,128)} %get-tuple-element.761, f32[128,8]{0,1:T(8,128)S(1)} %get-tuple-element.697, ...), kind=kOutput, calls=%fused_computation.32.clone.1 | convolution fusion | flops 137101312 | bytes 3350536 | tf_op jit(solution)/shard_map/while/body/eval_jaxpr/rhgk,khd->rhgd/dot_general | solution.py:36
  109.1 1.4 fusion.84
  110.5 2.6 %fusion.87 = f32[128,1,8,128]{0,3,2,1:T(8,128)} fusion(f32[512,128,8]{1,0,2:T(8,128)S(1)} %get-tuple-element.696, f32[128,8]{0,1:T(8,128)S(1)} %bitcast.261, pred[128,512]{0,1:T(8,128)(4,1)S(1)} %compare_and_fusion.2, f32[128,1,8,128]{0,3,2,1:T(8,128)} %get-tuple-element.761, f32[128,8]{0,1:T(8,128)S(1)} %get-tuple-element.697, ...), kind=kOutput, calls=%fused_computation.32.clone.1 | convolution fusion | flops 137101312 | bytes 3350536 | tf_op jit(solution)/shard_map/while/body/eval_jaxpr/rhgk,khd->rhgd/dot_general | solution.py:36
  113.8 1.4 fusion.84
  115.2 2.6 %fusion.87 = f32[128,1,8,128]{0,3,2,1:T(8,128)} fusion(f32[512,128,8]{1,0,2:T(8,128)S(1)} %get-tuple-element.696, f32[128,8]{0,1:T(8,128)S(1)} %bitcast.261, pred[128,512]{0,1:T(8,128)(4,1)S(1)} %compare_and_fusion.2, f32[128,1,8,128]{0,3,2,1:T(8,128)} %get-tuple-element.761, f32[128,8]{0,1:T(8,128)S(1)} %get-tuple-element.697, ...), kind=kOutput, calls=%fused_computation.32.clone.1 | convolution fusion | flops 137101312 | bytes 3350536 | tf_op jit(solution)/shard_map/while/body/eval_jaxpr/rhgk,khd->rhgd/dot_general | solution.py:36
  118.3 25.6 %all-gather.8.cloned.1.call-done = bf16[2,6144,1,128]{3,1,0,2:T(8,128)(2,1)} async-done(((bf16[2,384,1,128]{3,1,0,2:T(8,128)(2,1)}), bf16[2,6144,1,128]{3,1,0,2:T(8,128)(2,1)}) %all-gather.8.cloned.1.call-update) | async-done | bytes 3145744 | tf_op jit(solution)/shard_map/all_gather | solution.py:100
  143.9 2.6 %gather_fusion.2 = bf16[16,2,128,128]{3,2,1,0:T(8,128)(2,1)S(1)} fusion(bf16[2,48,128,128]{3,2,1,0:T(8,128)(2,1)} %bitcast.269, s32[1024]{0:T(1024)S(1)} %pad_clamp_fusion), kind=kCustom, calls=%fused_computation.2 | custom fusion | bytes 2097216 | tf_op jit(solution)/shard_map/gather | solution.py:107
  146.6 1.1 copy.67
  147.6 17.0 %while.55 = (s32[]{:T(128)}, f32[128,1,8]{0,2,1:T(8,128)S(1)}, f32[128,1,8]{0,2,1:T(8,128)S(1)}, f32[128,1,8,128]{0,3,2,1:T(8,128)}, bf16[2,2048,1,128]{3,1,2,0:...) while((s32[]{:T(128)}, f32[128,1,8]{0,2,1:T(8,128)S(1)}, ...), condition=%wide.region_14.15_spmd, body=%wide.region_11.14_spmd.sunk | while | flops 272894976 | bytes 7930035 | solution.py:55
  147.6 1.3 bitcast_reduce_fusion.2
  149.0 2.5 %fusion.82 = f32[128,1,8,128]{0,3,2,1:T(8,128)} fusion(f32[512,128,8]{1,0,2:T(8,128)S(1)} %get-tuple-element.684, f32[128,8]{0,1:T(8,128)S(1)} %bitcast.259, f32[128,1,8,128]{0,3,2,1:T(8,128)} %get-tuple-element.798, f32[128,8]{0,1:T(8,128)S(1)} %get-tuple-element.685, bf16[2,2048,1,128]{3,1,2,0:T(8,128)(2,1)} %get-tuple-element.810, s32[]{:T(128)S(6)} %add.337, ...), kind=kOutput, calls=%fused_computation.11.clone.1 | convolution fusion | flops 136052736 | bytes 3285000 | tf_op jit(solution)/shard_map/while/body/eval_jaxpr/rhgk,khd->rhgd/dot_general | solution.py:36
  151.9 1.4 bitcast_reduce_fusion.2
  153.2 2.5 %fusion.82 = f32[128,1,8,128]{0,3,2,1:T(8,128)} fusion(f32[512,128,8]{1,0,2:T(8,128)S(1)} %get-tuple-element.684, f32[128,8]{0,1:T(8,128)S(1)} %bitcast.259, f32[128,1,8,128]{0,3,2,1:T(8,128)} %get-tuple-element.798, f32[128,8]{0,1:T(8,128)S(1)} %get-tuple-element.685, bf16[2,2048,1,128]{3,1,2,0:T(8,128)(2,1)} %get-tuple-element.810, s32[]{:T(128)S(6)} %add.337, ...), kind=kOutput, calls=%fused_computation.11.clone.1 | convolution fusion | flops 136052736 | bytes 3285000 | tf_op jit(solution)/shard_map/while/body/eval_jaxpr/rhgk,khd->rhgd/dot_general | solution.py:36
  156.1 1.4 bitcast_reduce_fusion.2
  157.5 2.5 %fusion.82 = f32[128,1,8,128]{0,3,2,1:T(8,128)} fusion(f32[512,128,8]{1,0,2:T(8,128)S(1)} %get-tuple-element.684, f32[128,8]{0,1:T(8,128)S(1)} %bitcast.259, f32[128,1,8,128]{0,3,2,1:T(8,128)} %get-tuple-element.798, f32[128,8]{0,1:T(8,128)S(1)} %get-tuple-element.685, bf16[2,2048,1,128]{3,1,2,0:T(8,128)(2,1)} %get-tuple-element.810, s32[]{:T(128)S(6)} %add.337, ...), kind=kOutput, calls=%fused_computation.11.clone.1 | convolution fusion | flops 136052736 | bytes 3285000 | tf_op jit(solution)/shard_map/while/body/eval_jaxpr/rhgk,khd->rhgd/dot_general | solution.py:36
  160.4 1.4 bitcast_reduce_fusion.2
  161.7 2.5 %fusion.82 = f32[128,1,8,128]{0,3,2,1:T(8,128)} fusion(f32[512,128,8]{1,0,2:T(8,128)S(1)} %get-tuple-element.684, f32[128,8]{0,1:T(8,128)S(1)} %bitcast.259, f32[128,1,8,128]{0,3,2,1:T(8,128)} %get-tuple-element.798, f32[128,8]{0,1:T(8,128)S(1)} %get-tuple-element.685, bf16[2,2048,1,128]{3,1,2,0:T(8,128)(2,1)} %get-tuple-element.810, s32[]{:T(128)S(6)} %add.337, ...), kind=kOutput, calls=%fused_computation.11.clone.1 | convolution fusion | flops 136052736 | bytes 3285000 | tf_op jit(solution)/shard_map/while/body/eval_jaxpr/rhgk,khd->rhgd/dot_general | solution.py:36
  164.6 1.1 divide_convert_fusion
  166.0 17.8 %all_to_all.16 = bf16[8,16,1024]{2,1,0:T(8,128)(2,1)S(1)} all-to-all(bf16[8,16,1024]{2,1,0:T(8,128)(2,1)S(1)} %all_to_all.12), channel_id=1, replica_groups=mesh['mem'=16,'head'=8,'span'=4] {'head'}, dimensions={0} | all-to-all | bytes 524288 | tf_op jit(solution)/shard_map/all_to_all | solution.py:115
  184.0 0.8 broadcast_in_dim.170
  (98 shorter events, 8.8 us)
Async XLA Ops:
  6.5 11.0 %copy-start = (bf16[32,128,1,128]{3,1,2,0:T(8,128)(2,1)S(1)}, bf16[32,128,1,128]{3,1,2,0:T(8,128)(2,1)}, u32[]{:S(2)}) copy-start(bf16[32,128,1,128]{3,1,2,0:T(8,128)(2,1)} %param.15) | copy-start | bytes 3145732
  6.5 50.8 %all-gather.4.cloned.1.call-start = ((), (), s32[]{:S(2)}) async-start(), calls=%async_computation.1 | async-start | bytes 1114112 | tf_op jit(solution)/shard_map/all_gather | solution.py:78
  8.2 0.6 copy-start.1
  8.8 90.8 %all-gather.6.cloned.1.call-start = ((), (), s32[]{:S(2)}) async-start(), calls=%async_computation.2 | async-start | bytes 1114112 | tf_op jit(solution)/shard_map/all_gather | solution.py:81
  8.8 5.6 %collective-permute-start = (bf16[2,128,1,128]{3,1,2,0:T(8,128)(2,1)}, bf16[2,128,1,128]{3,1,2,0:T(8,128)(2,1)S(1)}, u32[]{:S(2)}, u32[]{:S(2)}) collective-permute-start(bf16[2,128,1,128]{3,1,2,0:T(8,128)(2,1)} %copy-done.1), channel_id=1, source_target_pairs={{0,1},{1,2},{2,3},{4,5},{5,6},{6,7},{8,9},{9,10},{10,11},{12,13},{... | collective-permute-start | bytes 196616 | tf_op jit(solution)/shard_map/ppermute | solution.py:13
  14.4 0.6 copy-start.2
  15.1 128.9 %all-gather.8.cloned.1.call-start = ((), (), s32[]{:S(2)}) async-start(), calls=%async_computation.3 | async-start | bytes 3342336 | tf_op jit(solution)/shard_map/all_gather | solution.py:100
Sparse Core Ops, SparseCore 0:
  9.5 47.7 all-gather.3
  59.4 40.0 all-gather.5
  101.7 42.1 all-gather.7
where the time goes:
time: 192 us; the launch traced here: 191 us
  waiting for transfers between devices  85.5 us (45%)
  matrix products  46.6 us (24%)
  blocking collectives  17.8 us (9%)
  between operations  13.2 us (7%)
  local copies, waits for them, and re-layouts  12.1 us (6%)
  other arithmetic  11.3 us (6%)
  starting transfers between devices  4.02 us (2%)
    all_gather x1, waiting for transfers between devices, local(): lax.all_gather(own_pair, 'mem', axis=1, tiled=True)  34.6 us
    dot_general x12, matrix products, update(): jnp.einsum('rhgk,khd->rhgd', weights.astype(jnp.bfloat16), key_pair[1], p...  30.3 us
    all_gather x1, waiting for transfers between devices, local(): gathered = lax.all_gather(block_pair, 'mem', axis=1, tiled=True)  25.6 us
    all_gather x1, waiting for transfers between devices, local(): lax.all_gather(prior_pair, 'mem', axis=1, tiled=True)  23.7 us
    all_to_all x1, blocking collectives, local(): lax.all_to_all(attended, 'head', split_axis=0, concat_axis=1, tiled=True)  17.8 us
    dot_general x12, matrix products, update(): jnp.einsum('rhgd,khd->rhgk', queries, key_pair[0], preferred_element_type...  16.3 us
    reduce_sum x12, other arithmetic, update(): new_total = old_total * factor + jnp.sum(weights, axis=-1)  5.5 us
    ppermute x1, starting transfers between devices, shifted(): lax.ppermute(value, axis, [(source, source + steps) for source in range(f...  3.94 us
  transfers between devices with their start and end apart: 4, of which 4 were waited for; matrix products, arithmetic and copies ran while one was open for 23% of the time, Pallas kernels for 0%

commit v1 on v0

--- a/solution.py
+++ b/solution.py
@@ -97,7 +97,9 @@
         per_head = [source_array[picked_units[0], :, 0, :]]
         gathered_pair.append(jnp.stack(per_head, axis=2))
     block_pair = jnp.stack(gathered_pair).reshape(2, capacity * unit_length, head_count, head_width)
-    gathered = lax.all_gather(block_pair, "mem", axis=1, tiled=True)
+    gathered = jnp.concatenate(
+        lax.all_to_all(jnp.stack([block_pair] * lax.axis_size("mem")), "mem", 0, 0), axis=1
+    )
     gathered = gathered.reshape(2, mem_count * capacity, unit_length, head_count, head_width)
     entry_range = jnp.arange(list_length, dtype=jnp.int32)
     earlier = entry_range[None, :] < entry_range[:, None]

time: 192 us -> 184 us (0.958)
  matrix products: 46.6 us -> 28.2 us
  starting transfers between devices: 4.02 us -> 15.4 us
  local copies, waits for them, and re-layouts: 12.1 us -> 18.6 us
  waiting for transfers between devices: 85.5 us -> 79.5 us
  other arithmetic: 11.3 us -> 8.97 us
    all_gather x1 -> x0, waiting for transfers between devices: 25.6 us -> none  [local(): gathered = lax.all_gather(block_pair, 'mem', axis=1, tiled=True)]
    all_gather x1, waiting for transfers between devices: 23.7 us -> 39.4 us  [local(): lax.all_gather(prior_pair, 'mem', axis=1, tiled=True)]
    dot_general x12, matrix products: 30.3 us -> 15.5 us  [update(): jnp.einsum('rhgk,khd->rhgd', weights.astype(jnp.bfloat16), key_pair[1], p...]
    all_to_all x0 -> x1, starting transfers between devices: none -> 11.4 us  [local(): lax.all_to_all(jnp.stack([block_pair] * lax.axis_size('mem')), 'mem', 0, 0)]
    all_gather x1, waiting for transfers between devices: 34.6 us -> 40.1 us  [local(): lax.all_gather(own_pair, 'mem', axis=1, tiled=True)]
    all_to_all x0 -> x1, local copies, waits for them, and re-layouts: none -> 3.93 us  [local(): lax.all_to_all(jnp.stack([block_pair] * lax.axis_size('mem')), 'mem', 0, 0)]
    dot_general x12, matrix products: 16.3 us -> 12.7 us  [update(): jnp.einsum('rhgd,khd->rhgk', queries, key_pair[0], preferred_element_type...]
    another operation x0 -> x1, local copies, waits for them, and re-layouts: none -> 2.41 us  [local(): jnp.stack([block_pair] * lax.axis_size('mem'))]
  transfers between devices with their start and end apart: 4 -> 4, of which waited for: 4 -> 2; matrix products, arithmetic and copies ran while one was open for 23% -> 20% of each run, Pallas kernels for 0% -> 0%
where the time goes in v1:
time: 184 us; the launch traced here: 183 us
  waiting for transfers between devices  79.5 us (43%)
  matrix products  28.2 us (15%)
  local copies, waits for them, and re-layouts  18.6 us (10%)
  blocking collectives  18.2 us (10%)
  starting transfers between devices  15.4 us (8%)
  between operations  13.6 us (7%)
  other arithmetic  8.97 us (5%)
    all_gather x1, waiting for transfers between devices, local(): lax.all_gather(own_pair, 'mem', axis=1, tiled=True)  40.1 us
    all_gather x1, waiting for transfers between devices, local(): lax.all_gather(prior_pair, 'mem', axis=1, tiled=True)  39.4 us
    all_to_all x1, blocking collectives, local(): lax.all_to_all(attended, 'head', split_axis=0, concat_axis=1, tiled=True)  18.2 us
    dot_general x12, matrix products, update(): jnp.einsum('rhgk,khd->rhgd', weights.astype(jnp.bfloat16), key_pair[1], p...  15.5 us
    dot_general x12, matrix products, update(): jnp.einsum('rhgd,khd->rhgk', queries, key_pair[0], preferred_element_type...  12.7 us
    all_to_all x1, starting transfers between devices, local(): lax.all_to_all(jnp.stack([block_pair] * lax.axis_size('mem')), 'mem', 0, 0)  11.4 us
    reduce_sum x12, other arithmetic, update(): new_total = old_total * factor + jnp.sum(weights, axis=-1)  5.51 us
    gather x2, local copies, waits for them, and re-layouts, local(): live_heads = [gathered[:, :, :, 0, :][:, slot_index[0]]]  4.85 us
  transfers between devices with their start and end apart: 4, of which 2 were waited for; matrix products, arithmetic and copies ran while one was open for 20% of the time, Pallas kernels for 0%

profile of v1, /device:TPU:1, one launch (start us, length us, event | category | flops | bytes accessed | tf_op | source)
XLA Modules:
  0.0 183.3 jit_solution(11340701454112443520)
XLA Ops:
  6.5 0.8 constant_dynamic-update-slice_fusion.1
  7.4 0.8 constant_dynamic-update-slice_fusion
  8.2 0.6 copy-done.2
  8.8 3.9 %collective-permute-start = (bf16[2,128,1,128]{3,1,2,0:T(8,128)(2,1)}, bf16[2,128,1,128]{3,1,2,0:T(8,128)(2,1)S(1)}, u32[]{:S(2)}, u32[]{:S(2)}) collective-permute-start(bf16[2,128,1,128]{3,1,2,0:T(8,128)(2,1)} %copy-done.2), channel_id=1, source_target_pairs={{0,1},{1,2},{2,3},{4,5},{5,6},{6,7},{8,9},{9,10},{10,11},{12,13},{... | collective-permute-start | bytes 196616 | tf_op jit(solution)/shard_map/ppermute | solution.py:13
  12.8 0.7 copy.79
  13.7 0.7 and_select_fusion.2
  14.3 0.7 broadcast_compare_fusion.1
  15.2 0.6 gather_fusion.1
  15.8 1.8 gather_fusion
  17.6 2.4 %stack.17 = bf16[16,2,384,1,128]{4,2,1,3,0:T(8,128)(2,1)} broadcast(bf16[2,384,128]{2,1,0:T(8,128)(2,1)S(1)} %maximum_bitcast_fusion), dimensions={1,2,4} | broadcast | bytes 3342336 | tf_op jit(solution)/shard_map/stack | solution.py:101
  20.0 11.4 %all-to-all-start = ((bf16[16,2,384,1,128]{4,2,1,3,0:T(8,128)(2,1)}), bf16[16,2,384,1,128]{4,2,1,3,0:T(8,128)(2,1)}, u32[]{:S(2)}, u32[]{:S(2)}) async-start(bf16[16,2,384,1,128]{4,2,1,3,0:T(8,128)(2,1)} %stack.17), calls=%async_computation | async-start | bytes 6291456 | tf_op jit(solution)/shard_map/all_to_all | solution.py:101
  32.0 0.6 copy-done.3
  32.6 40.1 %all-gather.3.cloned.1.call-done = bf16[2,2048,1,128]{3,1,2,0:T(8,128)(2,1)} async-done(((bf16[2,128,1,128]{3,1,2,0:T(8,128)(2,1)}), bf16[2,2048,1,128]{3,1,2,0:T(8,128)(2,1)}) %all-gather.3.cloned.1.call-update) | async-done | bytes 1048592 | tf_op jit(solution)/shard_map/all_gather | solution.py:78
  72.8 15.0 %while.57 = (s32[]{:T(128)}, f32[128,1,8]{0,2,1:T(8,128)S(1)}, f32[128,1,8]{0,2,1:T(8,128)S(1)}, f32[128,1,8,128]{0,3,2,1:T(8,128)S(1)}, bf16[2,2048,1,128]{3,1,...) while((s32[]{:T(128)}, f32[128,1,8]{0,2,1:T(8,128)S(1)}, ...), condition=%wide.region_3.4_spmd.clone, body=%wide.region_0.3_spmd.clone.sunk | while | flops 275716736 | bytes 8197335 | solution.py:55
  72.9 1.4 fusion.89
  74.3 0.5 fusion.91
  74.8 1.6 fusion.92
  76.7 1.4 fusion.89
  78.1 0.5 fusion.91
  78.6 1.6 fusion.92
  80.4 1.4 fusion.89
  81.8 0.5 fusion.91
  82.3 1.6 fusion.92
  84.2 1.4 fusion.89
  85.6 0.5 fusion.91
  86.1 1.6 fusion.92
  87.8 39.4 %all-gather.5.cloned.1.call-done = bf16[2,2048,1,128]{3,1,2,0:T(8,128)(2,1)} async-done(((bf16[2,128,1,128]{3,1,2,0:T(8,128)(2,1)}), bf16[2,2048,1,128]{3,1,2,0:T(8,128)(2,1)}) %all-gather.5.cloned.1.call-update) | async-done | bytes 1048592 | tf_op jit(solution)/shard_map/all_gather | solution.py:81
  127.1 15.0 %while.56 = (s32[]{:T(128)}, f32[128,1,8]{0,2,1:T(8,128)S(1)}, f32[128,1,8]{0,2,1:T(8,128)S(1)}, f32[128,1,8,128]{0,3,2,1:T(8,128)S(1)}, pred[]{:T(512)}, /*inde...) while((s32[]{:T(128)}, f32[128,1,8]{0,2,1:T(8,128)S(1)}, ...), condition=%wide.region_7.8_spmd.clone, body=%wide.region_4.7_spmd.clone.sunk | while | flops 275648128 | bytes 8197324 | solution.py:55
  127.3 1.4 fusion.84
  128.7 0.5 fusion.86
  129.2 1.6 fusion.87
  131.1 1.4 fusion.84
  132.4 0.5 fusion.86
  133.0 1.6 fusion.87
  134.8 1.4 fusion.84
  136.7 1.6 fusion.87
  138.6 1.4 fusion.84
  140.5 1.6 fusion.87
  142.2 3.9 %copy.85 = bf16[16,2,384,1,128]{4,2,0,1,3:T(8,128)(2,1)} copy(bf16[16,2,384,1,128]{4,2,1,3,0:T(8,128)(2,1)} %all-to-all-done) | data formatting | bytes 6291456 | tf_op jit(solution)/shard_map/all_to_all | solution.py:101
  146.1 3.6 %gather_fusion.2 = bf16[16,2,128,128]{3,2,1,0:T(8,128)(2,1)} fusion(bf16[2,48,128,128]{3,2,1,0:T(8,128)(2,1)} %bitcast.261, s32[1024]{0:T(1024)S(1)} %pad_clamp_fusion), kind=kCustom, calls=%fused_computation.2 | custom fusion | bytes 2097216 | tf_op jit(solution)/shard_map/gather | solution.py:109
  149.7 1.3 copy.87
  151.0 6.0 %while.55 = (s32[]{:T(128)}, f32[128,1,8]{0,2,1:T(8,128)S(1)}, f32[128,1,8]{0,2,1:T(8,128)S(1)}, f32[128,1,8,128]{0,3,2,1:T(8,128)S(1)}, bf16[2,2048,1,128]{3,1,...) while((s32[]{:T(128)}, f32[128,1,8]{0,2,1:T(8,128)S(1)}, ...), condition=%wide.region_14.15_spmd, body=%wide.region_11.14_spmd.sunk | while | flops 272894976 | bytes 7930035 | solution.py:55
  151.8 0.6 fusion.82
  153.3 0.6 fusion.82
  154.8 0.6 fusion.82
  156.3 0.6 fusion.82
  157.3 18.2 %all_to_all.21 = bf16[8,16,1024]{2,1,0:T(8,128)(2,1)S(1)} all-to-all(bf16[8,16,1024]{2,1,0:T(8,128)(2,1)S(1)} %all_to_all.16), channel_id=1, replica_groups=mesh['mem'=16,'head'=8,'span'=4] {'head'}, dimensions={0} | all-to-all | bytes 524288 | tf_op jit(solution)/shard_map/all_to_all | solution.py:117
  175.6 0.8 broadcast_in_dim.170
  (103 shorter events, 7.0 us)
Async XLA Ops:
  6.5 8.6 %copy-start = (bf16[32,128,1,128]{3,1,2,0:T(8,128)(2,1)S(1)}, bf16[32,128,1,128]{3,1,2,0:T(8,128)(2,1)}, u32[]{:S(2)}) copy-start(bf16[32,128,1,128]{3,1,2,0:T(8,128)(2,1)} %param.16) | copy-start | bytes 3145732
  6.5 66.2 %all-gather.3.cloned.1.call-start = ((), (), s32[]{:S(2)}) async-start(), calls=%async_computation.2 | async-start | bytes 1114112 | tf_op jit(solution)/shard_map/all_gather | solution.py:78
  8.2 0.6 copy-start.2
  8.8 23.2 %collective-permute-start = (bf16[2,128,1,128]{3,1,2,0:T(8,128)(2,1)}, bf16[2,128,1,128]{3,1,2,0:T(8,128)(2,1)S(1)}, u32[]{:S(2)}, u32[]{:S(2)}) collective-permute-start(bf16[2,128,1,128]{3,1,2,0:T(8,128)(2,1)} %copy-done.2), channel_id=1, source_target_pairs={{0,1},{1,2},{2,3},{4,5},{5,6},{6,7},{8,9},{9,10},{10,11},{12,13},{... | collective-permute-start | bytes 196616 | tf_op jit(solution)/shard_map/ppermute | solution.py:13
  20.0 11.5 %copy-start.4 = (s32[1,1,16]{2,1,0:T(1,128)S(1)}, s32[1,1,16]{2,1,0:T(1,128)}, u32[]{:S(2)}) copy-start(s32[1,1,16]{2,1,0:T(1,128)} %param.17) | copy-start | bytes 196
  20.0 11.8 %copy-start.1 = (bf16[1,128,1,8,128]{4,3,2,1,0:T(8,128)(2,1)S(1)}, bf16[1,128,1,8,128]{4,3,2,1,0:T(8,128)(2,1)}, u32[]{:S(2)}) copy-start(bf16[1,128,1,8,128]{4,3,2,1,0:T(8,128)(2,1)} %param.12) | copy-start | bytes 786436
  20.0 122.2 %all-to-all-start = ((bf16[16,2,384,1,128]{4,2,1,3,0:T(8,128)(2,1)}), bf16[16,2,384,1,128]{4,2,1,3,0:T(8,128)(2,1)}, u32[]{:S(2)}, u32[]{:S(2)}) async-start(bf16[16,2,384,1,128]{4,2,1,3,0:T(8,128)(2,1)} %stack.17), calls=%async_computation | async-start | bytes 6291456 | tf_op jit(solution)/shard_map/all_to_all | solution.py:101
  31.4 95.7 %all-gather.5.cloned.1.call-start = ((), (), s32[]{:S(2)}) async-start(), calls=%async_computation.3 | async-start | bytes 1114112 | tf_op jit(solution)/shard_map/all_gather | solution.py:81
  32.0 0.6 copy-start.3
Sparse Core Ops, SparseCore 0:
  9.5 63.2 all-gather.2
  74.9 52.1 all-gather.4
